TPU v7x, 32 devices: a whole 2x2x4 slice. The times are simulated.
32 devices in a mesh: row: 16 (over z, x, core), col: 2 (over y).
Axes of the slice: x: 2, y: 2, z: 4, core: 2. Of those that a mesh axis runs over, the one named last changes fastest.
Arguments:
- embeddings: bfloat16 [16384, 768], P(('row', 'col')), may hold values from -7.5 to 7.5
- block_cluster: int32 [64], replicated, may hold values from 0 to 15, never falling along the last dimension, each value on 1 to 8 neighbouring positions
- partner_shift: int32 [16384], P(('row', 'col')), may hold values from 1 to 255
Outputs:
- item_loss: float32 [16384], P(('row', 'col'))
- embedding_grad: float32 [16384, 768], P(('row', 'col'))
Inputs may be any that keep to these rules, and one draw needn't show every extreme that they name: block_cluster never falls along the blocks; each value is held by 1 to 8 consecutive blocks, and some value by exactly 8.
All inputs are finite; a program needn't handle non-finite values.
Results may differ from a plain program's by a relative error of at most 0.0018.
Values may be sent and summed in bfloat16 or wider, within the bound.
A program may use at most 128 MiB of HBM per device.

v0:
```python
import jax
import jax.numpy as jnp
from jax import lax
from jax.sharding import PartitionSpec as P

BLOCK = 256
REACH = 4


NEG = -1e30


def shifted(value, axis, steps):
    count = lax.axis_size(axis)
    leading, last = (max(0, -steps), min(count, count - steps))
    return lax.ppermute(value, axis, [(source, source + steps) for source in range(leading, last)])


def fetch_ahead(values, offset):
    return shifted(values, ("row", "col"), -offset)


def fetch_behind(values, offset):
    return shifted(values, ("row", "col"), offset)


def lse_ahead(values, offset):
    return shifted(values, ("row", "col"), -offset)


def lse_behind(values, offset):
    return shifted(values, ("row", "col"), offset)


def pair_scores(left, right, scale):
    return (
        lax.dot_general(left, right, (((1,), (1,)), ((), ())), preferred_element_type=jnp.float32)
        * scale
    )


def row_stats(scores, live):
    masked = jnp.where(live, scores, NEG)
    top = jnp.max(masked, axis=1)
    total = jnp.sum(jnp.where(live, jnp.exp(masked - top[:, None]), 0.0), axis=1)
    return (top, total)


def merge_stats(first, second):
    top = jnp.maximum(first[0], second[0])
    total = first[1] * jnp.exp(first[0] - top) + second[1] * jnp.exp(second[0] - top)
    return (top, total)


def tile_weights(scores, live, lse, far_lse):
    rowwise = jnp.exp(jnp.where(live, scores - lse[:, None], NEG))
    colwise = jnp.exp(jnp.where(live, scores - far_lse[None, :], NEG))
    return (rowwise + colwise).astype(jnp.bfloat16)


def shards(embeddings, block_cluster, partner_shift):
    rows = embeddings.shape[0]
    width = embeddings.shape[1]
    scale = width ** (-0.5)
    blocks_here = rows // BLOCK
    device = lax.axis_index(("row", "col"))
    margin = jnp.full((REACH * blocks_here,), -1, jnp.int32)
    beyond = jnp.full((REACH * blocks_here,), -2, jnp.int32)
    padded = jnp.concatenate([margin, block_cluster, beyond])
    start_block = device * blocks_here
    nearby = lax.dynamic_slice_in_dim(padded, start_block, (2 * REACH + 1) * blocks_here)

    def clusters_at(offset):
        begin = (REACH + offset) * blocks_here
        return jnp.repeat(nearby[begin : begin + blocks_here], BLOCK)

    mine = clusters_at(0)

    def live_at(offset):
        return mine[:, None] == clusters_at(offset)[None, :]

    position = jnp.arange(rows, dtype=jnp.int32)
    diagonal = position[:, None] == position[None, :]
    live_self = live_at(0) & jnp.logical_not(diagonal)
    within = position % BLOCK
    partner = position - within + (within + partner_shift) % BLOCK
    positive = position[None, :] == partner[:, None]
    self_scores = pair_scores(embeddings, embeddings, scale)
    stats = row_stats(self_scores, live_self)
    ahead_tiles = []
    behind_tiles = []
    for offset in range(1, REACH + 1):
        ahead = fetch_ahead(embeddings, offset)
        live = live_at(offset)
        scores = pair_scores(embeddings, ahead, scale)
        stats = merge_stats(stats, row_stats(scores, live))
        ahead_tiles.append((ahead, scores, live))
        behind = fetch_behind(embeddings, offset)
        live_back = live_at(-offset)
        scores_back = pair_scores(embeddings, behind, scale)
        stats = merge_stats(stats, row_stats(scores_back, live_back))
        behind_tiles.append((behind, scores_back, live_back))
    lse = stats[0] + jnp.log(stats[1])
    item_loss = lse - jnp.sum(jnp.where(positive, self_scores, 0.0), axis=1)
    self_terms = jnp.exp(jnp.where(live_self, self_scores - lse[:, None], NEG)) - positive.astype(
        jnp.float32
    )
    self_weights = (self_terms + self_terms.T).astype(jnp.bfloat16)
    grad = jnp.dot(self_weights, embeddings, preferred_element_type=jnp.float32) * scale
    for offset in range(1, REACH + 1):
        ahead, scores, live = ahead_tiles[offset - 1]
        far_lse = lse_ahead(lse, offset)
        weights = tile_weights(scores, live, lse, far_lse)
        grad = grad + jnp.dot(weights, ahead, preferred_element_type=jnp.float32) * scale
        behind, scores_back, live_back = behind_tiles[offset - 1]
        back_lse = lse_behind(lse, offset)
        weights_back = tile_weights(scores_back, live_back, lse, back_lse)
        grad = grad + jnp.dot(weights_back, behind, preferred_element_type=jnp.float32) * scale
    return (item_loss, grad)


def solution(mesh):
    in_specs = (P(("row", "col"), None), P(), P(("row", "col")))
    out_specs = (P(("row", "col")), P(("row", "col"), None))
    return jax.shard_map(shards, mesh=mesh, in_specs=in_specs, out_specs=out_specs, check_vma=False)
```

profile of v0, /device:TPU:16, one launch (start us, length us, event | category | flops | bytes accessed | tf_op | source)
XLA Modules:
  0.0 147.8 jit_solution(15221742721079412816)
XLA Ops:
  0.6 3.7 %collective-permute-start = (bf16[512,768]{1,0:T(8,128)(2,1)}, bf16[512,768]{1,0:T(8,128)(2,1)}, u32[]{:S(2)}, u32[]{:S(2)}) collective-permute-start(bf16[512,768]{1,0:T(8,128)(2,1)} %param.3), channel_id=1, source_target_pairs={{1,0},{2,1},{3,2},{4,3},{5,4},{6,5},{7,6},{8,7},{9,8},{10,9},{11,1... | collective-permute-start | bytes 2359304 | tf_op jit(solution)/shard_map/ppermute | solution.py:16
  4.3 2.8 %collective-permute-start.2 = (bf16[512,768]{1,0:T(8,128)(2,1)}, bf16[512,768]{1,0:T(8,128)(2,1)}, u32[]{:S(2)}, u32[]{:S(2)}) collective-permute-start(bf16[512,768]{1,0:T(8,128)(2,1)} %param.3), channel_id=1, source_target_pairs={{2,0},{3,1},{4,2},{5,3},{6,4},{7,5},{8,6},{9,7},{10,8},{11,9},{12,... | collective-permute-start | bytes 2359304 | tf_op jit(solution)/shard_map/ppermute | solution.py:16
  9.0 2.6 %collective-permute-start.4 = (bf16[512,768]{1,0:T(8,128)(2,1)}, bf16[512,768]{1,0:T(8,128)(2,1)}, u32[]{:S(2)}, u32[]{:S(2)}) collective-permute-start(bf16[512,768]{1,0:T(8,128)(2,1)} %param.3), channel_id=1, source_target_pairs={{3,0},{4,1},{5,2},{6,3},{7,4},{8,5},{9,6},{10,7},{11,8},{12,9},{13... | collective-permute-start | bytes 2359304 | tf_op jit(solution)/shard_map/ppermute | solution.py:16
  11.7 2.9 %collective-permute-start.5 = (bf16[512,768]{1,0:T(8,128)(2,1)}, bf16[512,768]{1,0:T(8,128)(2,1)}, u32[]{:S(2)}, u32[]{:S(2)}) collective-permute-start(bf16[512,768]{1,0:T(8,128)(2,1)} %param.3), channel_id=1, source_target_pairs={{0,3},{1,4},{2,5},{3,6},{4,7},{5,8},{6,9},{7,10},{8,11},{9,12},{10... | collective-permute-start | bytes 2359304 | tf_op jit(solution)/shard_map/ppermute | solution.py:16
  14.6 2.1 %convolution_multiply_fusion.8 = f32[512,512]{0,1:T(8,128)S(1)} fusion(bf16[512,768]{1,0:T(8,128)(2,1)} %param.3), kind=kOutput, calls=%fused_computation.41 | convolution fusion | flops 402915328 | bytes 1835008 | tf_op jit(solution)/shard_map/dot_general | solution.py:37
  17.8 13.2 %collective-permute-done.2 = bf16[512,768]{1,0:T(8,128)(2,1)} collective-permute-done((bf16[512,768]{1,0:T(8,128)(2,1)}, bf16[512,768]{1,0:T(8,128)(2,1)}, u32[]{:S(2)}, u32[]{:S(2)}) %collective-permute-start.2) | collective-permute-done | bytes 786464 | tf_op jit(solution)/shard_map/ppermute | solution.py:16
  31.1 19.3 %collective-permute-start.6 = (bf16[512,768]{1,0:T(8,128)(2,1)S(1)}, bf16[512,768]{1,0:T(8,128)(2,1)S(1)}, u32[]{:S(2)}, u32[]{:S(2)}) collective-permute-start(bf16[512,768]{1,0:T(8,128)(2,1)S(1)} %copy-done), channel_id=1, source_target_pairs={{4,0},{5,1},{6,2},{7,3},{8,4},{9,5},{10,6},{11,7},{12,8},{13,9},{1... | collective-permute-start | bytes 2359304 | tf_op jit(solution)/shard_map/ppermute | solution.py:16
  52.1 2.0 %collective-permute-start.7 = (bf16[512,768]{1,0:T(8,128)(2,1)S(1)}, bf16[512,768]{1,0:T(8,128)(2,1)S(1)}, u32[]{:S(2)}, u32[]{:S(2)}) collective-permute-start(bf16[512,768]{1,0:T(8,128)(2,1)S(1)} %copy-done), channel_id=1, source_target_pairs={{0,4},{1,5},{2,6},{3,7},{4,8},{5,9},{6,10},{7,11},{8,12},{9,13},{1... | collective-permute-start | bytes 2359304 | tf_op jit(solution)/shard_map/ppermute | solution.py:16
  59.7 2.1 %convolution_multiply_fusion.3 = f32[512,512]{1,0:T(8,128)S(1)} fusion(bf16[512,768]{1,0:T(8,128)(2,1)S(1)} %copy-done, bf16[512,768]{1,0:T(8,128)(2,1)} %collective-permute-done.4), kind=kOutput, calls=%fused_computation.36 | convolution fusion | flops 402915328 | bytes 2621440 | tf_op jit(solution)/shard_map/dot_general | solution.py:37
  61.8 2.1 %convolution_multiply_fusion.2 = f32[512,512]{1,0:T(8,128)S(1)} fusion(bf16[512,768]{1,0:T(8,128)(2,1)S(1)} %copy-done, bf16[512,768]{1,0:T(8,128)(2,1)} %collective-permute-done.5), kind=kOutput, calls=%fused_computation.35 | convolution fusion | flops 402915328 | bytes 2621440 | tf_op jit(solution)/shard_map/dot_general | solution.py:37
  64.7 26.4 %collective-permute-done.6 = bf16[512,768]{1,0:T(8,128)(2,1)S(1)} collective-permute-done((bf16[512,768]{1,0:T(8,128)(2,1)S(1)}, bf16[512,768]{1,0:T(8,128)(2,1)S(1)}, u32[]{:S(2)}, u32[]{:S(2)}) %collective-permute-start.6) | collective-permute-done | bytes 786464 | tf_op jit(solution)/shard_map/ppermute | solution.py:16
  95.9 2.1 %fusion.5 = (f32[512]{0:T(512)S(1)}, f32[512]{0:T(512)S(1)}, f32[512]{0:T(512)S(1)}, f32[512]{0:T(512)S(1)}, f32[512]{0:T(512)S(1)}, /*index=5*/f32[512]{0:T(512)S(1)}) fusion(f32[512,512]{1,0:T(8,128)S(1)} %get-tuple-element.32, f32[512]{0:T(512)S(1)} %get-tuple-element.4, s32[512]{0:T(512)S(1)} %bitcast.83, s32[512]{0:T(512)S(1)} %bitcast.69, ...), kind=kLoop, calls=%fused_computation.47 | loop fusion | flops 7861248 | bytes 6330368 | tf_op jit(solution)/shard_map/reduce_sum | solution.py:45
  98.6 3.7 %collective-permute-start.14 = (f32[512]{0:T(512)S(1)}, f32[512]{0:T(512)S(1)}, u32[]{:S(2)}, u32[]{:S(2)}) collective-permute-start(f32[512]{0:T(512)S(1)} %get-tuple-element.20), channel_id=1, source_target_pairs={{4,0},{5,1},{6,2},{7,3},{8,4},{9,5},{10,6},{11,7},{12,8},{13,9},{1... | collective-permute-start | bytes 6152 | tf_op jit(solution)/shard_map/ppermute | solution.py:16
  104.2 5.7 %collective-permute-start.12 = (f32[512]{0:T(512)S(1)}, f32[512]{0:T(512)S(1)}, u32[]{:S(2)}, u32[]{:S(2)}) collective-permute-start(f32[512]{0:T(512)S(1)} %get-tuple-element.20), channel_id=1, source_target_pairs={{3,0},{4,1},{5,2},{6,3},{7,4},{8,5},{9,6},{10,7},{11,8},{12,9},{13... | collective-permute-start | bytes 6152 | tf_op jit(solution)/shard_map/ppermute | solution.py:16
  111.9 4.5 %collective-permute-start.10 = (f32[512]{0:T(512)S(1)}, f32[512]{0:T(512)S(1)}, u32[]{:S(2)}, u32[]{:S(2)}) collective-permute-start(f32[512]{0:T(512)S(1)} %get-tuple-element.20), channel_id=1, source_target_pairs={{2,0},{3,1},{4,2},{5,3},{6,4},{7,5},{8,6},{9,7},{10,8},{11,9},{12,... | collective-permute-start | bytes 6152 | tf_op jit(solution)/shard_map/ppermute | solution.py:16
  117.6 2.5 %copy.17 = f32[512,512]{1,0:T(8,128)} copy(f32[512,512]{0,1:T(8,128)} %broadcast_subtract_fusion) | data formatting | bytes 2097152 | tf_op jit(solution)/shard_map/sub | solution.py:105
  120.1 3.0 %fusion.58 = f32[512,768]{1,0:T(8,128)S(1)} fusion(bf16[512,768]{1,0:T(8,128)(2,1)S(1)} %copy-done, f32[512,512]{0,1:T(8,128)} %broadcast_subtract_fusion, f32[512,512]{1,0:T(8,128)} %copy.17, s32[512]{0:T(512)S(1)} %fusion.126, s32[512]{0:T(512)S(1)} %bitcast.70), kind=kOutput, calls=%fused_computation.107 | convolution fusion | flops 407371776 | bytes 4460544 | tf_op jit(solution)/shard_map/dot_general | solution.py:109
  123.2 3.0 %collective-permute-start.9 = (f32[512]{0:T(512)S(1)}, f32[512]{0:T(512)S(1)}, u32[]{:S(2)}, u32[]{:S(2)}) collective-permute-start(f32[512]{0:T(512)S(1)} %get-tuple-element.20), channel_id=1, source_target_pairs={{0,1},{1,2},{2,3},{3,4},{4,5},{5,6},{6,7},{7,8},{8,9},{9,10},{10,1... | collective-permute-start | bytes 6152 | tf_op jit(solution)/shard_map/ppermute | solution.py:16
  127.1 4.6 %collective-permute-start.8 = (f32[512]{0:T(512)S(1)}, f32[512]{0:T(512)S(1)}, u32[]{:S(2)}, u32[]{:S(2)}) collective-permute-start(f32[512]{0:T(512)S(1)} %get-tuple-element.20), channel_id=1, source_target_pairs={{1,0},{2,1},{3,2},{4,3},{5,4},{6,5},{7,6},{8,7},{9,8},{10,9},{11,1... | collective-permute-start | bytes 6152 | tf_op jit(solution)/shard_map/ppermute | solution.py:16
  131.7 2.0 %fusion.66 = f32[512,768]{1,0:T(8,128)S(1)} fusion(bf16[512,768]{1,0:T(8,128)(2,1)} %collective-permute-done.5, f32[512,512]{1,0:T(8,128)S(1)} %copy-done.6, f32[512]{0:T(512)S(1)} %collective-permute-done.13, f32[512]{0:T(512)S(1)} %get-tuple-element.20, s32[512]{0:T(512)S(1)} %bitcast.93, s32[512]{0:T(512)S(1)} %bitcast.72), kind=kOutput, calls=%fused_computation.110 | convolution fusion | flops 404488192 | bytes 3416064 | tf_op jit(solution)/shard_map/dot_general | solution.py:118
  133.8 2.2 %collective-permute-start.15 = (f32[512]{0:T(512)S(1)}, f32[512]{0:T(512)S(1)}, u32[]{:S(2)}, u32[]{:S(2)}) collective-permute-start(f32[512]{0:T(512)S(1)} %get-tuple-element.20), channel_id=1, source_target_pairs={{0,4},{1,5},{2,6},{3,7},{4,8},{5,9},{6,10},{7,11},{8,12},{9,13},{1... | collective-permute-start | bytes 6152 | tf_op jit(solution)/shard_map/ppermute | solution.py:16
  138.0 2.1 %fusion.70 = f32[512,768]{1,0:T(8,128)S(1)} fusion(bf16[512,768]{1,0:T(8,128)(2,1)} %collective-permute-done.3, f32[512,512]{1,0:T(8,128)S(1)} %copy-done.10, f32[512]{0:T(512)S(1)} %collective-permute-done.11, f32[512]{0:T(512)S(1)} %get-tuple-element.20, s32[512]{0:T(512)S(1)} %bitcast.99, s32[512]{0:T(512)S(1)} %bitcast.74), kind=kOutput, calls=%fused_computation.112 | convolution fusion | flops 404488192 | bytes 3416064 | tf_op jit(solution)/shard_map/dot_general | solution.py:118
  140.2 2.1 %fusion.72 = f32[512,768]{1,0:T(8,128)S(1)} fusion(bf16[512,768]{1,0:T(8,128)(2,1)} %collective-permute-done.2, f32[512,512]{1,0:T(8,128)S(1)} %copy-done.2, f32[512]{0:T(512)S(1)} %collective-permute-done.10, f32[512]{0:T(512)S(1)} %get-tuple-element.20, s32[512]{0:T(512)S(1)} %bitcast.87, s32[512]{0:T(512)S(1)} %bitcast.75), kind=kOutput, calls=%fused_computation.113 | convolution fusion | flops 404488192 | bytes 3416064 | tf_op jit(solution)/shard_map/dot_general | solution.py:114
  145.6 2.3 %add_multiply_fusion = f32[512,768]{1,0:T(8,128)} fusion(f32[512,768]{1,0:T(8,128)S(1)} %fusion.64, f32[512,768]{1,0:T(8,128)S(1)} %fusion.66, f32[512,768]{1,0:T(8,128)S(1)} %fusion.68, f32[512,768]{1,0:T(8,128)S(1)} %fusion.70, f32[512,768]{1,0:T(8,128)S(1)} %fusion.72, f32[512,768]{1,0:T(8,128)S(1)} %fusion.74, f32[512,768]{1,0:T(8,128)S(1)} %fusion.58, ...), kind=kOutput, calls=%fused_computation.32 | convolution fusion | flops 408027136 | bytes 15998976 | tf_op jit(solution)/shard_map/dot_general | solution.py:118
  (103 shorter events, 27.2 us)
Async XLA Ops:
  0.6 16.2 %copy-start.22 = (s32[64]{0:T(128)S(1)}, s32[64]{0:T(128)}, u32[]{:S(2)}) copy-start(s32[64]{0:T(128)} %param.4) | copy-start | bytes 772
  0.6 55.3 %collective-permute-start = (bf16[512,768]{1,0:T(8,128)(2,1)}, bf16[512,768]{1,0:T(8,128)(2,1)}, u32[]{:S(2)}, u32[]{:S(2)}) collective-permute-start(bf16[512,768]{1,0:T(8,128)(2,1)} %param.3), channel_id=1, source_target_pairs={{1,0},{2,1},{3,2},{4,3},{5,4},{6,5},{7,6},{8,7},{9,8},{10,9},{11,1... | collective-permute-start | bytes 2359304 | tf_op jit(solution)/shard_map/ppermute | solution.py:16
  4.3 26.7 %collective-permute-start.2 = (bf16[512,768]{1,0:T(8,128)(2,1)}, bf16[512,768]{1,0:T(8,128)(2,1)}, u32[]{:S(2)}, u32[]{:S(2)}) collective-permute-start(bf16[512,768]{1,0:T(8,128)(2,1)} %param.3), channel_id=1, source_target_pairs={{2,0},{3,1},{4,2},{5,3},{6,4},{7,5},{8,6},{9,7},{10,8},{11,9},{12,... | collective-permute-start | bytes 2359304 | tf_op jit(solution)/shard_map/ppermute | solution.py:16
  7.1 45.0 %collective-permute-start.3 = (bf16[512,768]{1,0:T(8,128)(2,1)}, bf16[512,768]{1,0:T(8,128)(2,1)}, u32[]{:S(2)}, u32[]{:S(2)}) collective-permute-start(bf16[512,768]{1,0:T(8,128)(2,1)} %param.3), channel_id=1, source_target_pairs={{0,2},{1,3},{2,4},{3,5},{4,6},{5,7},{6,8},{7,9},{8,10},{9,11},{10,... | collective-permute-start | bytes 2359304 | tf_op jit(solution)/shard_map/ppermute | solution.py:16
  9.0 50.7 %collective-permute-start.4 = (bf16[512,768]{1,0:T(8,128)(2,1)}, bf16[512,768]{1,0:T(8,128)(2,1)}, u32[]{:S(2)}, u32[]{:S(2)}) collective-permute-start(bf16[512,768]{1,0:T(8,128)(2,1)} %param.3), channel_id=1, source_target_pairs={{3,0},{4,1},{5,2},{6,3},{7,4},{8,5},{9,6},{10,7},{11,8},{12,9},{13... | collective-permute-start | bytes 2359304 | tf_op jit(solution)/shard_map/ppermute | solution.py:16
  11.7 50.2 %collective-permute-start.5 = (bf16[512,768]{1,0:T(8,128)(2,1)}, bf16[512,768]{1,0:T(8,128)(2,1)}, u32[]{:S(2)}, u32[]{:S(2)}) collective-permute-start(bf16[512,768]{1,0:T(8,128)(2,1)} %param.3), channel_id=1, source_target_pairs={{0,3},{1,4},{2,5},{3,6},{4,7},{5,8},{6,9},{7,10},{8,11},{9,12},{10... | collective-permute-start | bytes 2359304 | tf_op jit(solution)/shard_map/ppermute | solution.py:16
  16.7 14.3 %copy-start = (bf16[512,768]{1,0:T(8,128)(2,1)S(1)}, bf16[512,768]{1,0:T(8,128)(2,1)}, u32[]{:S(2)}) copy-start(bf16[512,768]{1,0:T(8,128)(2,1)} %param.3) | copy-start | bytes 2359300
  17.7 46.3 %copy-start.11 = (f32[512,512]{1,0:T(8,128)}, f32[512,512]{1,0:T(8,128)S(1)}, u32[]{:S(2)}) copy-start(f32[512,512]{1,0:T(8,128)S(1)} %copy.6) | copy-start | bytes 3145732
  31.1 60.0 %collective-permute-start.6 = (bf16[512,768]{1,0:T(8,128)(2,1)S(1)}, bf16[512,768]{1,0:T(8,128)(2,1)S(1)}, u32[]{:S(2)}, u32[]{:S(2)}) collective-permute-start(bf16[512,768]{1,0:T(8,128)(2,1)S(1)} %copy-done), channel_id=1, source_target_pairs={{4,0},{5,1},{6,2},{7,3},{8,4},{9,5},{10,6},{11,7},{12,8},{13,9},{1... | collective-permute-start | bytes 2359304 | tf_op jit(solution)/shard_map/ppermute | solution.py:16
  52.1 43.7 %copy-start.1 = (f32[512,512]{1,0:T(8,128)}, f32[512,512]{1,0:T(8,128)S(1)}, u32[]{:S(2)}) copy-start(f32[512,512]{1,0:T(8,128)S(1)} %convolution_multiply_fusion.5) | copy-start | bytes 3145732
  52.1 39.6 %collective-permute-start.7 = (bf16[512,768]{1,0:T(8,128)(2,1)S(1)}, bf16[512,768]{1,0:T(8,128)(2,1)S(1)}, u32[]{:S(2)}, u32[]{:S(2)}) collective-permute-start(bf16[512,768]{1,0:T(8,128)(2,1)S(1)} %copy-done), channel_id=1, source_target_pairs={{0,4},{1,5},{2,6},{3,7},{4,8},{5,9},{6,10},{7,11},{8,12},{9,13},{1... | collective-permute-start | bytes 2359304 | tf_op jit(solution)/shard_map/ppermute | solution.py:16
  55.9 39.5 %copy-start.9 = (f32[512,512]{1,0:T(8,128)}, f32[512,512]{1,0:T(8,128)S(1)}, u32[]{:S(2)}) copy-start(f32[512,512]{1,0:T(8,128)S(1)} %convolution_multiply_fusion.4) | copy-start | bytes 3145732
  55.9 36.4 %collective-permute-start.1 = (bf16[512,768]{1,0:T(8,128)(2,1)S(1)}, bf16[512,768]{1,0:T(8,128)(2,1)S(1)}, u32[]{:S(2)}, u32[]{:S(2)}) collective-permute-start(bf16[512,768]{1,0:T(8,128)(2,1)S(1)} %copy-done), channel_id=1, source_target_pairs={{0,1},{1,2},{2,3},{3,4},{4,5},{5,6},{6,7},{7,8},{8,9},{9,10},{10,1... | collective-permute-start | bytes 2359304 | tf_op jit(solution)/shard_map/ppermute | solution.py:16
  61.8 34.0 %copy-start.3 = (f32[512,512]{1,0:T(8,128)}, f32[512,512]{1,0:T(8,128)S(1)}, u32[]{:S(2)}) copy-start(f32[512,512]{1,0:T(8,128)S(1)} %convolution_multiply_fusion.3) | copy-start | bytes 3145732
  64.0 31.9 %copy-start.5 = (f32[512,512]{1,0:T(8,128)}, f32[512,512]{1,0:T(8,128)S(1)}, u32[]{:S(2)}) copy-start(f32[512,512]{1,0:T(8,128)S(1)} %convolution_multiply_fusion.2) | copy-start | bytes 3145732
  98.6 24.5 %collective-permute-start.14 = (f32[512]{0:T(512)S(1)}, f32[512]{0:T(512)S(1)}, u32[]{:S(2)}, u32[]{:S(2)}) collective-permute-start(f32[512]{0:T(512)S(1)} %get-tuple-element.20), channel_id=1, source_target_pairs={{4,0},{5,1},{6,2},{7,3},{8,4},{9,5},{10,6},{11,7},{12,8},{13,9},{1... | collective-permute-start | bytes 6152 | tf_op jit(solution)/shard_map/ppermute | solution.py:16
  102.3 24.8 %collective-permute-start.13 = (f32[512]{0:T(512)S(1)}, f32[512]{0:T(512)S(1)}, u32[]{:S(2)}, u32[]{:S(2)}) collective-permute-start(f32[512]{0:T(512)S(1)} %get-tuple-element.20), channel_id=1, source_target_pairs={{0,3},{1,4},{2,5},{3,6},{4,7},{5,8},{6,9},{7,10},{8,11},{9,12},{10... | collective-permute-start | bytes 6152 | tf_op jit(solution)/shard_map/ppermute | solution.py:16
  104.2 29.5 %collective-permute-start.12 = (f32[512]{0:T(512)S(1)}, f32[512]{0:T(512)S(1)}, u32[]{:S(2)}, u32[]{:S(2)}) collective-permute-start(f32[512]{0:T(512)S(1)} %get-tuple-element.20), channel_id=1, source_target_pairs={{3,0},{4,1},{5,2},{6,3},{7,4},{8,5},{9,6},{10,7},{11,8},{12,9},{13... | collective-permute-start | bytes 6152 | tf_op jit(solution)/shard_map/ppermute | solution.py:16
  110.0 28.1 %collective-permute-start.11 = (f32[512]{0:T(512)S(1)}, f32[512]{0:T(512)S(1)}, u32[]{:S(2)}, u32[]{:S(2)}) collective-permute-start(f32[512]{0:T(512)S(1)} %get-tuple-element.20), channel_id=1, source_target_pairs={{0,2},{1,3},{2,4},{3,5},{4,6},{5,7},{6,8},{7,9},{8,10},{9,11},{10,... | collective-permute-start | bytes 6152 | tf_op jit(solution)/shard_map/ppermute | solution.py:16
  111.9 28.3 %collective-permute-start.10 = (f32[512]{0:T(512)S(1)}, f32[512]{0:T(512)S(1)}, u32[]{:S(2)}, u32[]{:S(2)}) collective-permute-start(f32[512]{0:T(512)S(1)} %get-tuple-element.20), channel_id=1, source_target_pairs={{2,0},{3,1},{4,2},{5,3},{6,4},{7,5},{8,6},{9,7},{10,8},{11,9},{12,... | collective-permute-start | bytes 6152 | tf_op jit(solution)/shard_map/ppermute | solution.py:16
  123.2 19.2 %collective-permute-start.9 = (f32[512]{0:T(512)S(1)}, f32[512]{0:T(512)S(1)}, u32[]{:S(2)}, u32[]{:S(2)}) collective-permute-start(f32[512]{0:T(512)S(1)} %get-tuple-element.20), channel_id=1, source_target_pairs={{0,1},{1,2},{2,3},{3,4},{4,5},{5,6},{6,7},{7,8},{8,9},{9,10},{10,1... | collective-permute-start | bytes 6152 | tf_op jit(solution)/shard_map/ppermute | solution.py:16
  127.1 8.9 %copy-start.4 = (f32[512,512]{1,0:T(8,128)S(1)}, f32[512,512]{1,0:T(8,128)}, u32[]{:S(2)}) copy-start(f32[512,512]{1,0:T(8,128)} %copy-done.3) | copy-start | bytes 3145732
  127.1 16.1 %collective-permute-start.8 = (f32[512]{0:T(512)S(1)}, f32[512]{0:T(512)S(1)}, u32[]{:S(2)}, u32[]{:S(2)}) collective-permute-start(f32[512]{0:T(512)S(1)} %get-tuple-element.20), channel_id=1, source_target_pairs={{1,0},{2,1},{3,2},{4,3},{5,4},{6,5},{7,6},{8,7},{9,8},{10,9},{11,1... | collective-permute-start | bytes 6152 | tf_op jit(solution)/shard_map/ppermute | solution.py:16
  133.8 11.8 %collective-permute-start.15 = (f32[512]{0:T(512)S(1)}, f32[512]{0:T(512)S(1)}, u32[]{:S(2)}, u32[]{:S(2)}) collective-permute-start(f32[512]{0:T(512)S(1)} %get-tuple-element.20), channel_id=1, source_target_pairs={{0,4},{1,5},{2,6},{3,7},{4,8},{5,9},{6,10},{7,11},{8,12},{9,13},{1... | collective-permute-start | bytes 6152 | tf_op jit(solution)/shard_map/ppermute | solution.py:16
  (17 other events, 54.3 us)
where the time goes:
time: 150 us; the launch traced here: 148 us
  starting transfers between devices  64.8 us (43%)
  waiting for transfers between devices  39.7 us (26%)
  matrix products  31.8 us (21%)
  local copies, waits for them, and re-layouts  5.15 us (3%)
  other arithmetic  5.07 us (3%)
    ppermute x16, starting transfers between devices, shifted(): lax.ppermute(value, axis, [(source, source + steps) for source in range(l...  64.8 us
    ppermute x16, waiting for transfers between devices, shifted(): lax.ppermute(value, axis, [(source, source + steps) for source in range(l...  39.7 us
    dot_general x9, matrix products, pair_scores(): lax.dot_general(left, right, (((1,), (1,)), ((), ())), preferred_element_...  14.5 us
    dot_general x4, matrix products, shards(): jnp.dot(weights_back, behind, preferred_element_type=jnp.float32) * scale  7.24 us
    dot_general x4, matrix products, shards(): jnp.dot(weights, ahead, preferred_element_type=jnp.float32) * scale  6.99 us
    dot_general x1, matrix products, shards(): jnp.dot(self_weights, embeddings, preferred_element_type=jnp.float32)  3.02 us
  transfers between devices with their start and end apart: 16, of which 2 were waited for; matrix products, arithmetic and copies ran while one was open for 22% of the time, Pallas kernels for 0%

commit v1 on v0

v1 whole, which is shorter than its diff:
```python
import functools

import jax
import jax.numpy as jnp
from jax import lax
from jax.experimental import pallas as pl
from jax.experimental.pallas import tpu as pltpu
from jax.sharding import PartitionSpec as P

BLOCK = 256
REACH = 4
CHUNK = 128
NEG = -1e30
F32 = jnp.float32


def kernel(
    row_axis, col_axis, devices, cols, scale,
    live_ref, e_ref, qcol_ref, qrow_ref,
    grad_ref, loss_ref,
    buf, scores, weights, top, total, lse_col, lse_send, lse_far, pos_score,
    recv, xs, ys, cs, zs, ls, lr,
):
    me = lax.axis_index(row_axis) * cols + lax.axis_index(col_axis)
    y = me % 2
    c = me // 2 % 2
    x = me // 4 % 2
    g = 2 * c + y
    gy = 2 * c + 1 - y
    gp = 2 * (1 - c) + y
    gpy = 2 * (1 - c) + 1 - y
    oth = 32 * (1 - x)
    adj = 32 * x
    xpeer = me + 4 - 8 * x
    ypeer = me + 1 - 2 * y
    cpeer = me + 2 - 4 * c
    zto = me + 8 - 16 * x
    zfrom = me - 8 + 16 * x
    z_send = (zto >= 0) & (zto < devices)
    z_recv = (zfrom >= 0) & (zfrom < devices)

    def at(device):
        return (device // cols, device % cols)

    def exists(device):
        return (device >= 0) & (device < devices)

    barrier = pltpu.get_barrier_semaphore()
    count = jnp.int32(0)
    for offset in (-8, -4, -3, -2, -1, 1, 2, 3, 4, 8):
        there = exists(me + offset)
        count = count + there.astype(jnp.int32)

        @pl.when(there)
        def _():
            pl.semaphore_signal(
                barrier, inc=1, device_id=at(me + offset), device_id_type=pl.DeviceIdType.MESH
            )
    pl.semaphore_wait(barrier, count)

    def rows(slot):
        return buf.at[pl.ds(pl.multiple_of(slot * CHUNK, CHUNK), CHUNK), :]

    def remote(src, slot, send, device):
        return pltpu.make_async_remote_copy(
            src_ref=src, dst_ref=rows(slot), send_sem=send, recv_sem=recv.at[slot],
            device_id=at(device), device_id_type=pl.DeviceIdType.MESH,
        )

    def own(i):
        return e_ref.at[pl.ds(i * CHUNK, CHUNK), :]

    def x_own(i):
        return remote(own(i), adj + 4 * g + i, xs.at[i], xpeer)

    def y_own(i):
        return remote(own(i), 16 + 4 * g + i, ys.at[i], ypeer)

    def c_own(i):
        return remote(own(i), 16 + 4 * g + i, cs.at[16 + 4 * g + i], cpeer)

    def x_relay(i):
        return remote(rows(16 + 4 * gy + i), adj + 4 * gy + i, xs.at[4 + i], xpeer)

    def y_relay(i):
        return remote(rows(oth + 4 * g + i), oth + 4 * g + i, ys.at[2 + i], ypeer)

    def z_need(r):
        return jnp.where(x == 0, r >= 4 * y + 2, r <= 4 * y + 9)

    def z_relay(r):
        return remote(rows(oth + r), adj + r, zs.at[r], zto)

    def c_relay(slot):
        return remote(rows(slot), slot, cs.at[slot], cpeer)

    def c_gives(slot):
        return (slot >= 4 * gp + 2) & (slot <= 4 * gp + 33)

    def c_takes(slot):
        return (slot >= 4 * g + 2) & (slot <= 4 * g + 33)

    def arrived(slot):
        remote(rows(slot), slot, zs.at[0], cpeer).wait_recv()

    def when(cond, action):
        pl.when(cond)(action)

    for i in range(4):
        x_own(i).start()
        y_own(i).start()
        c_own(i).start()

    when(~z_recv, lambda: buf.__setitem__(
        (pl.ds(pl.multiple_of(adj * CHUNK, CHUNK), 16 * CHUNK), slice(None)),
        jnp.zeros((16 * CHUNK, buf.shape[1]), buf.dtype)))
    for offset in (-4, -3, -2, -1, 1, 2, 3, 4):
        when(~exists(me + offset), lambda: lse_far.__setitem__(
            offset + 4, jnp.zeros(lse_far.shape[1:], F32)))

    n = e_ref.shape[0]

    half = lax.broadcasted_iota(jnp.int32, (n, BLOCK), 0)
    lane = lax.broadcasted_iota(jnp.int32, (n, BLOCK), 1)
    q = qcol_ref[...]
    own_scores = []
    for h in range(2):
        s = lax.dot_general(
            e_ref[...], e_ref[h * BLOCK:(h + 1) * BLOCK, :], (((1,), (1,)), ((), ())),
            preferred_element_type=F32) * scale
        cell = lane + h * BLOCK
        hit = jnp.sum(jnp.where(q == cell, s, 0.0), axis=1, keepdims=True)
        own_scores.append((s, hit))
        ok = jnp.concatenate(
            [jnp.full((BLOCK, BLOCK), live_ref[7 + h, r], jnp.int32) for r in range(2)], 0) > 0
        scores[7 + h] = jnp.where(ok & (half != cell), s, NEG)
    buf[pl.ds(pl.multiple_of((16 + 4 * g) * CHUNK, 4 * CHUNK), n), :] = e_ref[...]
    pos_score[...] = own_scores[0][1] + own_scores[1][1]
    m = jnp.maximum(jnp.max(scores[7], axis=1, keepdims=True), jnp.max(scores[8], axis=1, keepdims=True))
    top[...] = m
    total[...] = jnp.sum(jnp.exp(scores[7] - m), axis=1, keepdims=True) + jnp.sum(
        jnp.exp(scores[8] - m), axis=1, keepdims=True)

    def process(block):
        k = block - (2 * g + 1)

        @pl.when((k >= 0) & (k < 16))
        def _():
            far = buf[pl.ds(pl.multiple_of(block * BLOCK, BLOCK), BLOCK), :]
            for r in range(2):
                part = pl.ds(r * BLOCK, BLOCK)
                s = lax.dot_general(
                    e_ref[part, :], far, (((1,), (1,)), ((), ())),
                    preferred_element_type=F32) * scale
                s = jnp.where(live_ref[k, r] > 0, s, NEG)
                scores[k, part, :] = s
                old = top[part, :]
                new = jnp.maximum(old, jnp.max(s, axis=1, keepdims=True))
                total[part, :] = total[part, :] * jnp.exp(old - new) + jnp.sum(
                    jnp.exp(s - new), axis=1, keepdims=True)
                top[part, :] = new

    def give(slot, also=True):
        when(c_gives(slot) & also, lambda: c_relay(slot).start())

    def event(kind, i):
        if kind == "X":
            slot = oth + 4 * g + i
            arrived(slot)
            when(z_send & z_need(4 * g + i), lambda: z_relay(4 * g + i).start())
            if i >= 2:
                y_relay(i).start()
            give(slot)
        elif kind == "Y":
            slot = 16 + 4 * gy + i
            arrived(slot)
            if i < 2:
                x_relay(i).start()
            give(slot)
        elif kind == "D":
            slot = oth + 4 * gy + i
            arrived(slot)
            when(z_send & z_need(4 * gy + i), lambda: z_relay(4 * gy + i).start())
            give(slot)
        else:
            e = 4 * (g if kind == "Z" else gy) + i

            def take():
                arrived(adj + e)
                give(adj + e)
            when(z_recv & z_need(e), take)

    def c_wait(base, cond=True):
        for i in range(4):
            when(c_takes(base + i) & cond, lambda: arrived(base + i))

    steps = [
        ([("X", 0), ("Y", 0), ("X", 1), ("Y", 1)], (16 + 4 * gp, "own"), 16 + 4 * gp),
        ([("X", 2), ("Y", 2), ("Z", 0), ("X", 3), ("Y", 3), ("Z", 1)], None, oth + 4 * g),
        ([], None, 16 + 4 * gy),
        ([("D", 0), ("D", 2), ("Z", 2)], (16 + 4 * gpy, True), 16 + 4 * gpy),
        ([("D", 1), ("D", 3), ("Z", 3)], (oth + 4 * gp, True), oth + 4 * gp),
        ([], None, oth + 4 * gy),
        ([("W", 0), ("W", 2)], (oth + 4 * gpy, True), oth + 4 * gpy),
        ([("W", 1), ("W", 3)], None, adj + 4 * g),
        ([], (adj + 4 * gp, z_recv), adj + 4 * gp),
        ([], None, adj + 4 * gy),
        ([], (adj + 4 * gpy, z_recv), adj + 4 * gpy),
    ]

    def step(u, carry):
        base = jnp.int32(0)
        for index, (events, cwait, slot) in enumerate(steps):
            base = base + jnp.where(u == index, slot, 0)
            if events or cwait is not None:
                @pl.when(u == index)
                def _():
                    for kind, i in events:
                        event(kind, i)
                    if cwait is not None:
                        if cwait[1] == "own":
                            for i in range(4):
                                arrived(cwait[0] + i)
                        else:
                            c_wait(*cwait)
        for h in range(2):
            process(base // 2 + h)
        return carry

    lax.fori_loop(0, len(steps), step, 0)

    lse = top[...] + jnp.log(total[...])
    lse_col[...] = lse
    loss = lse - pos_score[...]
    both = jnp.where(
        lax.broadcasted_iota(jnp.int32, (n, 128), 1) < 8,
        jnp.broadcast_to(lse, (n, 128)), jnp.broadcast_to(loss, (n, 128)))
    turned = both.T
    lse_send[...] = turned[:8, :]
    lse_far[4] = turned[:8, :]
    loss_ref[...] = turned[8:9, :]

    def lse_copy(offset):
        return pltpu.make_async_remote_copy(
            src_ref=lse_send, dst_ref=lse_far.at[4 - offset],
            send_sem=ls.at[4 + offset], recv_sem=lr.at[4 - offset],
            device_id=at(me + offset), device_id_type=pl.DeviceIdType.MESH,
        )

    for offset in (-4, 4, -3, 3, -2, 2, -1, 1):
        when(exists(me + offset), lambda: lse_copy(offset).start())

    def fill(k):
        offset = (k - 7) // 2
        h = (k - 7) % 2
        s = scores[k]
        w = jnp.exp(s - lse_col[...]) + jnp.exp(
            s - lse_far[offset + 4][0:1, h * BLOCK:(h + 1) * BLOCK])
        if offset == 0:
            cell = lax.broadcasted_iota(jnp.int32, (n, BLOCK), 1) + h * BLOCK
            line = lax.broadcasted_iota(jnp.int32, (n, BLOCK), 0)
            w = w - (qcol_ref[...] == cell).astype(F32)
            w = w - (qrow_ref[0:1, h * BLOCK:(h + 1) * BLOCK] == line).astype(F32)
        weights[:, k * BLOCK:(k + 1) * BLOCK] = w.astype(jnp.bfloat16)

    fill(7)
    fill(8)
    for offset in (-1, 1, -2, 2, -3, 3, -4, 4):
        when(exists(me + offset), lambda: lse_copy(-offset).wait_recv())
        for k in range(16):
            if (k - 7) // 2 == offset:
                fill(k)

    width = e_ref.shape[1]

    def product(t, carry):
        columns = pl.ds(pl.multiple_of(t * 256, 256), 256)
        near = buf[pl.ds(pl.multiple_of((2 * g + 1) * BLOCK, BLOCK), 16 * BLOCK), columns]
        grad_ref[:, columns] = jnp.dot(weights[...], near, preferred_element_type=F32) * scale
        return carry

    lax.fori_loop(0, width // 256, product, 0)

    for offset in (-4, 4, -3, 3, -2, 2, -1, 1):
        when(exists(me + offset), lambda: lse_copy(offset).wait_send())
    for i in range(4):
        x_own(i).wait_send()
        y_own(i).wait_send()
        c_own(i).wait_send()
        when(z_send & z_need(4 * g + i), lambda: z_relay(4 * g + i).wait_send())
        when(z_send & z_need(4 * gy + i), lambda: z_relay(4 * gy + i).wait_send())
        for slot in (oth + 4 * g + i, 16 + 4 * gy + i, oth + 4 * gy + i):
            when(c_gives(slot), lambda: c_relay(slot).wait_send())
        for e in (4 * g + i, 4 * gy + i):
            when(c_gives(adj + e) & z_recv & z_need(e), lambda: c_relay(adj + e).wait_send())
        if i < 2:
            x_relay(i).wait_send()
        else:
            y_relay(i).wait_send()


def solution(mesh):
    row_axis, col_axis = mesh.axis_names
    devices = mesh.shape[row_axis] * mesh.shape[col_axis]
    cols = mesh.shape[col_axis]

    def shards(embeddings, block_cluster, partner_shift):
        rows, width = embeddings.shape
        blocks = rows // BLOCK
        device = lax.axis_index((row_axis, col_axis))
        margin = jnp.full((7,), -1, jnp.int32)
        beyond = jnp.full((8,), -2, jnp.int32)
        padded = jnp.concatenate([margin, block_cluster, beyond])
        window = lax.dynamic_slice_in_dim(padded, device * blocks, 16)
        live = (window[:, None] == window[None, 7:9]).astype(jnp.int32)
        position = jnp.arange(rows, dtype=jnp.int32)
        within = position % BLOCK
        partner = position - within + (within + partner_shift) % BLOCK
        vmem = pl.BlockSpec(memory_space=pltpu.VMEM)
        grad, loss = pl.pallas_call(
            functools.partial(kernel, row_axis, col_axis, devices, cols, width ** (-0.5)),
            out_shape=(
                jax.ShapeDtypeStruct((rows, width), F32),
                jax.ShapeDtypeStruct((1, rows), F32),
            ),
            in_specs=[pl.BlockSpec(memory_space=pltpu.SMEM), vmem, vmem, vmem],
            out_specs=(vmem, vmem),
            scratch_shapes=[
                pltpu.VMEM((24 * BLOCK, width), jnp.bfloat16),
                pltpu.VMEM((16, rows, BLOCK), F32),
                pltpu.VMEM((rows, 16 * BLOCK), jnp.bfloat16),
                pltpu.VMEM((rows, 1), F32),
                pltpu.VMEM((rows, 1), F32),
                pltpu.VMEM((rows, 1), F32),
                pltpu.VMEM((8, rows), F32),
                pltpu.VMEM((2 * REACH + 1, 8, rows), F32),
                pltpu.VMEM((rows, 1), F32),
                pltpu.SemaphoreType.DMA((48,)),
                pltpu.SemaphoreType.DMA((6,)),
                pltpu.SemaphoreType.DMA((6,)),
                pltpu.SemaphoreType.DMA((48,)),
                pltpu.SemaphoreType.DMA((16,)),
                pltpu.SemaphoreType.DMA((2 * REACH + 1,)),
                pltpu.SemaphoreType.DMA((2 * REACH + 1,)),
            ],
            compiler_params=pltpu.CompilerParams(
                collective_id=0, has_side_effects=True, vmem_limit_bytes=60 * 1024 * 1024
            ),
        )(live, embeddings, partner[:, None], partner[None, :])
        return loss.reshape(rows), grad

    in_specs = (P((row_axis, col_axis), None), P(), P((row_axis, col_axis)))
    out_specs = (P((row_axis, col_axis)), P((row_axis, col_axis), None))
    return jax.shard_map(shards, mesh=mesh, in_specs=in_specs, out_specs=out_specs, check_vma=False)
```

time: 150 us -> 71 us (0.47)
  the two profiles are of different devices: /device:TPU:16 before, /device:TPU:15 now
where the time goes in v1:
time: 71 us; the launch traced here: 70.8 us
  Pallas kernels  63.1 us (89%)
  local copies, waits for them, and re-layouts  4.91 us (7%)
  other arithmetic  2.09 us (3%)
    pallas_call x1, Pallas kernels, shards(): pl.pallas_call(functools.partial(kernel, row_axis, col_axis, devices, col...  63.1 us
    unnamed x4, local copies, waits for them, and re-layouts  3.9 us

profile of v1, /device:TPU:15, one launch (start us, length us, event | category | flops | bytes accessed | tf_op | source)
XLA Modules:
  0.0 70.8 jit_solution(5199628971972657508)
XLA Ops:
  0.7 0.7 %pad_add_fusion = s32[79]{0:T(128)S(1)} fusion(s32[8]{0:T(128)S(1)} %broadcast.17, s32[64]{0:T(128)} %param.4, s32[7]{0:T(128)S(1)} %broadcast.16), kind=kLoop, calls=%fused_computation.13 | loop fusion | flops 158 | bytes 632 | tf_op jit(solution)/shard_map/concatenate | solution.py:313
  1.4 0.1 dynamic_slice.3
  1.5 0.1 slice.3
  1.5 0.7 fusion.3
  2.2 0.0 copy-start
  2.2 0.7 compare_convert_fusion.live_ref
  2.9 0.9 %copy.5.qcol_ref = s32[512,1]{1,0:T(8,128)} copy(s32[512,1]{0,1:T(1,128)S(1)} %bitcast.3) | data formatting | bytes 4096 | tf_op jit(solution)/shard_map/broadcast_in_dim | solution.py:349
  3.8 0.0 copy-done
  3.8 63.1 %shard_map.50 = (f32[512,768]{1,0:T(8,128)}, f32[1,512]{1,0:T(1,128)}) custom-call(s32[16,2]{1,0:T(8,128)} %compare_convert_fusion.live_ref, bf16[512,768]{1,0:T(8,128)(2,1)} %e_ref.1, s32[512,1]{1,0:T(8,128)} %copy.5.qcol_ref, s32[1,512]{1,0:T(1,128)} %bitcast.4), custom_call_target="tpu_custom_call" | custom-call | tf_op jit(solution)/shard_map/pallas_call | solution.py:320
  66.9 1.2 %copy.8 = f32[512]{0:T(512)} copy(f32[512]{0:T(512)} %bitcast.5) | data formatting | bytes 4096
  68.1 2.7 %copy.9 = f32[512,768]{1,0:T(8,128)} copy(f32[512,768]{1,0:T(8,128)} %get-tuple-element.9) | data formatting | bytes 3145728
  (2 shorter events, 0.0 us)
Async XLA Ops:
  2.2 1.5 %copy-start = (s32[512]{0:T(512)}, s32[512]{0:T(512)S(1)}, u32[]{:S(2)}) copy-start(s32[512]{0:T(512)S(1)} %fusion.3) | copy-start | bytes 6148

commit v2 on v1

--- a/solution.py
+++ b/solution.py
@@ -16,9 +16,9 @@
 
 def kernel(
     row_axis, col_axis, devices, cols, scale,
-    live_ref, e_ref, qcol_ref, qrow_ref,
+    cluster_ref, e_ref, shift_ref,
     grad_ref, loss_ref,
-    buf, scores, weights, top, total, lse_col, lse_send, lse_far, pos_score,
+    buf, scores, weights, top, total, lse_col, lse_send, lse_far, pos_score, qcol_ref, qrow_ref,
     recv, xs, ys, cs, zs, ls, lr,
 ):
     me = lax.axis_index(row_axis) * cols + lax.axis_index(col_axis)
@@ -91,6 +91,16 @@
     def z_relay(r):
         return remote(rows(oth + r), adj + r, zs.at[r], zto)
 
+    zy_send = z_recv & (c == 0) & (y == 1 - x)
+    zy_skip = (c == 0) & (y == x)
+
+    def z_gives(i):
+        need = z_send & z_need(4 * gy + i)
+        return need & ~zy_skip if i >= 2 else need
+
+    def zy_relay(i):
+        return remote(rows(adj + 4 * g + i), adj + 4 * g + i, ys.at[4 + i], ypeer)
+
     def c_relay(slot):
         return remote(rows(slot), slot, cs.at[slot], cpeer)
 
@@ -106,9 +116,10 @@
     def when(cond, action):
         pl.when(cond)(action)
 
+    for i in range(2):
+        x_own(2 + i).start()
+        y_own(i).start()
     for i in range(4):
-        x_own(i).start()
-        y_own(i).start()
         c_own(i).start()
 
     when(~z_recv, lambda: buf.__setitem__(
@@ -119,6 +130,19 @@
             offset + 4, jnp.zeros(lse_far.shape[1:], F32)))
 
     n = e_ref.shape[0]
+    blocks = cluster_ref.shape[0]
+
+    def alive(k, r):
+        there = 2 * me + k - 7
+        near = jnp.maximum(jnp.minimum(there, blocks - 1), 0)
+        same = cluster_ref[near] == cluster_ref[2 * me + r]
+        return same & (there == near)
+
+    place = lax.broadcasted_iota(jnp.int32, (1, n), 1)
+    within = place % BLOCK
+    goal = place - within + (within + shift_ref[...]) % BLOCK
+    qrow_ref[...] = goal
+    qcol_ref[...] = jnp.broadcast_to(goal.astype(F32), (128, n)).T[:, :1].astype(jnp.int32)
 
     half = lax.broadcasted_iota(jnp.int32, (n, BLOCK), 0)
     lane = lax.broadcasted_iota(jnp.int32, (n, BLOCK), 1)
@@ -132,7 +156,7 @@
         hit = jnp.sum(jnp.where(q == cell, s, 0.0), axis=1, keepdims=True)
         own_scores.append((s, hit))
         ok = jnp.concatenate(
-            [jnp.full((BLOCK, BLOCK), live_ref[7 + h, r], jnp.int32) for r in range(2)], 0) > 0
+            [jnp.full((BLOCK, BLOCK), alive(7 + h, r).astype(jnp.int32), jnp.int32) for r in range(2)], 0) > 0
         scores[7 + h] = jnp.where(ok & (half != cell), s, NEG)
     buf[pl.ds(pl.multiple_of((16 + 4 * g) * CHUNK, 4 * CHUNK), n), :] = e_ref[...]
     pos_score[...] = own_scores[0][1] + own_scores[1][1]
@@ -152,7 +176,7 @@
                 s = lax.dot_general(
                     e_ref[part, :], far, (((1,), (1,)), ((), ())),
                     preferred_element_type=F32) * scale
-                s = jnp.where(live_ref[k, r] > 0, s, NEG)
+                s = jnp.where(alive(k, r), s, NEG)
                 scores[k, part, :] = s
                 old = top[part, :]
                 new = jnp.maximum(old, jnp.max(s, axis=1, keepdims=True))
@@ -170,61 +194,67 @@
             when(z_send & z_need(4 * g + i), lambda: z_relay(4 * g + i).start())
             if i >= 2:
                 y_relay(i).start()
+                y_own(i).start()
             give(slot)
         elif kind == "Y":
             slot = 16 + 4 * gy + i
             arrived(slot)
             if i < 2:
                 x_relay(i).start()
+                x_own(i).start()
             give(slot)
         elif kind == "D":
             slot = oth + 4 * gy + i
             arrived(slot)
-            when(z_send & z_need(4 * gy + i), lambda: z_relay(4 * gy + i).start())
+            when(z_gives(i), lambda: z_relay(4 * gy + i).start())
             give(slot)
         else:
             e = 4 * (g if kind == "Z" else gy) + i
 
             def take():
                 arrived(adj + e)
+                if kind == "Z" and i >= 2:
+                    when(zy_send, lambda: zy_relay(i).start())
                 give(adj + e)
             when(z_recv & z_need(e), take)
 
-    def c_wait(base, cond=True):
-        for i in range(4):
-            when(c_takes(base + i) & cond, lambda: arrived(base + i))
-
+    def c_wait(block, cond):
+        for i in range(2):
+            when(c_takes(2 * block + i) & cond, lambda: arrived(2 * block + i))
+
+    def at_block(base, element, h):
+        return base // 2 + 2 * element + h
+
+    here = jnp.int32(16)
     steps = [
-        ([("X", 0), ("Y", 0), ("X", 1), ("Y", 1)], (16 + 4 * gp, "own"), 16 + 4 * gp),
-        ([("X", 2), ("Y", 2), ("Z", 0), ("X", 3), ("Y", 3), ("Z", 1)], None, oth + 4 * g),
-        ([], None, 16 + 4 * gy),
-        ([("D", 0), ("D", 2), ("Z", 2)], (16 + 4 * gpy, True), 16 + 4 * gpy),
-        ([("D", 1), ("D", 3), ("Z", 3)], (oth + 4 * gp, True), oth + 4 * gp),
-        ([], None, oth + 4 * gy),
-        ([("W", 0), ("W", 2)], (oth + 4 * gpy, True), oth + 4 * gpy),
-        ([("W", 1), ("W", 3)], None, adj + 4 * g),
-        ([], (adj + 4 * gp, z_recv), adj + 4 * gp),
-        ([], None, adj + 4 * gy),
-        ([], (adj + 4 * gpy, z_recv), adj + 4 * gpy),
+        ([("X", 2), ("Y", 0)], [(at_block(here, gp, 0), True), (at_block(here, gp, 1), True)]),
+        ([("X", 3), ("Y", 1), ("Z", 2)], [(at_block(oth, g, 1), None), (at_block(here, gy, 0), None)]),
+        ([("D", 0), ("D", 2), ("Z", 3)], [(at_block(oth, gp, 1), True), (at_block(here, gpy, 0), True)]),
+        ([("X", 0), ("Y", 2), ("W", 0)], [(at_block(adj, g, 1), None), (at_block(adj, gp, 1), z_recv)]),
+        ([("D", 1), ("D", 3), ("W", 2)], [(at_block(oth, gy, 0), None), (at_block(oth, gy, 1), None)]),
+        ([("X", 1), ("Y", 3), ("Z", 0)], [(at_block(oth, g, 0), None), (at_block(here, gy, 1), None)]),
+        ([("W", 1)], [(at_block(oth, gp, 0), True), (at_block(here, gpy, 1), True)]),
+        ([("W", 3)], [(at_block(oth, gpy, 0), True), (at_block(oth, gpy, 1), True)]),
+        ([("Z", 1)], [(at_block(adj, gy, 0), None), (at_block(adj, gy, 1), None)]),
+        ([], [(at_block(adj, gpy, 0), z_recv), (at_block(adj, gpy, 1), z_recv)]),
+        ([], [(at_block(adj, g, 0), None), (at_block(adj, gp, 0), z_recv)]),
     ]
 
     def step(u, carry):
-        base = jnp.int32(0)
-        for index, (events, cwait, slot) in enumerate(steps):
-            base = base + jnp.where(u == index, slot, 0)
-            if events or cwait is not None:
-                @pl.when(u == index)
-                def _():
-                    for kind, i in events:
-                        event(kind, i)
-                    if cwait is not None:
-                        if cwait[1] == "own":
-                            for i in range(4):
-                                arrived(cwait[0] + i)
-                        else:
-                            c_wait(*cwait)
+        spots = [jnp.int32(0), jnp.int32(0)]
+        for index, (events, ready) in enumerate(steps):
+            for h in range(2):
+                spots[h] = spots[h] + jnp.where(u == index, ready[h][0], 0)
+
+            @pl.when(u == index)
+            def _():
+                for kind, i in events:
+                    event(kind, i)
+                for block, cond in ready:
+                    if cond is not None:
+                        c_wait(block, cond)
         for h in range(2):
-            process(base // 2 + h)
+            process(spots[h])
         return carry
 
     lax.fori_loop(0, len(steps), step, 0)
@@ -288,7 +318,7 @@
         y_own(i).wait_send()
         c_own(i).wait_send()
         when(z_send & z_need(4 * g + i), lambda: z_relay(4 * g + i).wait_send())
-        when(z_send & z_need(4 * gy + i), lambda: z_relay(4 * gy + i).wait_send())
+        when(z_gives(i), lambda: z_relay(4 * gy + i).wait_send())
         for slot in (oth + 4 * g + i, 16 + 4 * gy + i, oth + 4 * gy + i):
             when(c_gives(slot), lambda: c_relay(slot).wait_send())
         for e in (4 * g + i, 4 * gy + i):
@@ -297,6 +327,7 @@
             x_relay(i).wait_send()
         else:
             y_relay(i).wait_send()
+            when(zy_send, lambda: zy_relay(i).wait_send())
 
 
 def solution(mesh):
@@ -306,16 +337,6 @@
 
     def shards(embeddings, block_cluster, partner_shift):
         rows, width = embeddings.shape
-        blocks = rows // BLOCK
-        device = lax.axis_index((row_axis, col_axis))
-        margin = jnp.full((7,), -1, jnp.int32)
-        beyond = jnp.full((8,), -2, jnp.int32)
-        padded = jnp.concatenate([margin, block_cluster, beyond])
-        window = lax.dynamic_slice_in_dim(padded, device * blocks, 16)
-        live = (window[:, None] == window[None, 7:9]).astype(jnp.int32)
-        position = jnp.arange(rows, dtype=jnp.int32)
-        within = position % BLOCK
-        partner = position - within + (within + partner_shift) % BLOCK
         vmem = pl.BlockSpec(memory_space=pltpu.VMEM)
         grad, loss = pl.pallas_call(
             functools.partial(kernel, row_axis, col_axis, devices, cols, width ** (-0.5)),
@@ -323,7 +344,7 @@
                 jax.ShapeDtypeStruct((rows, width), F32),
                 jax.ShapeDtypeStruct((1, rows), F32),
             ),
-            in_specs=[pl.BlockSpec(memory_space=pltpu.SMEM), vmem, vmem, vmem],
+            in_specs=[pl.BlockSpec(memory_space=pltpu.SMEM), vmem, vmem],
             out_specs=(vmem, vmem),
             scratch_shapes=[
                 pltpu.VMEM((24 * BLOCK, width), jnp.bfloat16),
@@ -335,9 +356,11 @@
                 pltpu.VMEM((8, rows), F32),
                 pltpu.VMEM((2 * REACH + 1, 8, rows), F32),
                 pltpu.VMEM((rows, 1), F32),
+                pltpu.VMEM((rows, 1), jnp.int32),
+                pltpu.VMEM((1, rows), jnp.int32),
                 pltpu.SemaphoreType.DMA((48,)),
                 pltpu.SemaphoreType.DMA((6,)),
-                pltpu.SemaphoreType.DMA((6,)),
+                pltpu.SemaphoreType.DMA((8,)),
                 pltpu.SemaphoreType.DMA((48,)),
                 pltpu.SemaphoreType.DMA((16,)),
                 pltpu.SemaphoreType.DMA((2 * REACH + 1,)),
@@ -346,7 +369,7 @@
             compiler_params=pltpu.CompilerParams(
                 collective_id=0, has_side_effects=True, vmem_limit_bytes=60 * 1024 * 1024
             ),
-        )(live, embeddings, partner[:, None], partner[None, :])
+        )(block_cluster, embeddings, partner_shift.reshape(1, rows))
         return loss.reshape(rows), grad
 
     in_specs = (P((row_axis, col_axis), None), P(), P((row_axis, col_axis)))

time: 71 us -> 62.2 us (0.88)
  the two profiles are of different devices: /device:TPU:15 before, /device:TPU:16 now
where the time goes in v2:
time: 62.2 us; the launch traced here: 61.7 us
  Pallas kernels  57.2 us (92%)
  local copies, waits for them, and re-layouts  3.9 us (6%)
  between operations  0.64 us (1%)
    pallas_call x1, Pallas kernels, shards(): pl.pallas_call(functools.partial(kernel, row_axis, col_axis, devices, col...  57.2 us
    unnamed x2, local copies, waits for them, and re-layouts  3.9 us

profile of v2, /device:TPU:16, one launch (start us, length us, event | category | flops | bytes accessed | tf_op | source)
XLA Modules:
  0.0 61.7 jit_solution(3454217074732473145)
XLA Ops:
  0.6 57.2 %shard_map.50 = (f32[512,768]{1,0:T(8,128)}, f32[1,512]{1,0:T(1,128)}) custom-call(s32[64]{0:T(128)} %cluster_ref.1, bf16[512,768]{1,0:T(8,128)(2,1)} %e_ref.1, s32[1,512]{1,0:T(1,128)} %bitcast.2), custom_call_target="tpu_custom_call" | custom-call | tf_op jit(solution)/shard_map/pallas_call | solution.py:341
  57.8 1.3 %copy.7 = f32[512]{0:T(512)} copy(f32[512]{0:T(512)} %bitcast.3) | data formatting | bytes 4096
  59.1 2.7 %copy.8 = f32[512,768]{1,0:T(8,128)} copy(f32[512,768]{1,0:T(8,128)} %get-tuple-element.9) | data formatting | bytes 3145728

commit v3 on v2

--- a/solution.py
+++ b/solution.py
@@ -235,9 +235,9 @@
         ([("X", 1), ("Y", 3), ("Z", 0)], [(at_block(oth, g, 0), None), (at_block(here, gy, 1), None)]),
         ([("W", 1)], [(at_block(oth, gp, 0), True), (at_block(here, gpy, 1), True)]),
         ([("W", 3)], [(at_block(oth, gpy, 0), True), (at_block(oth, gpy, 1), True)]),
-        ([("Z", 1)], [(at_block(adj, gy, 0), None), (at_block(adj, gy, 1), None)]),
+        ([], [(at_block(adj, gy, 0), None), (at_block(adj, gy, 1), None)]),
         ([], [(at_block(adj, gpy, 0), z_recv), (at_block(adj, gpy, 1), z_recv)]),
-        ([], [(at_block(adj, g, 0), None), (at_block(adj, gp, 0), z_recv)]),
+        ([("Z", 1)], [(at_block(adj, g, 0), None), (at_block(adj, gp, 0), z_recv)]),
     ]
 
     def step(u, carry):
@@ -367,7 +367,7 @@
                 pltpu.SemaphoreType.DMA((2 * REACH + 1,)),
             ],
             compiler_params=pltpu.CompilerParams(
-                collective_id=0, has_side_effects=True, vmem_limit_bytes=60 * 1024 * 1024
+                collective_id=0, has_side_effects=True, vmem_limit_bytes=34 * 1024 * 1024
             ),
         )(block_cluster, embeddings, partner_shift.reshape(1, rows))
         return loss.reshape(rows), grad

time: 62.2 us -> 58.5 us (0.941)
  Pallas kernels: 57.2 us -> 53.5 us
    pallas_call x1, Pallas kernels: 57.2 us -> 53.5 us  [shards(): pl.pallas_call(functools.partial(kernel, row_axis, col_axis, devices, col...]
    unnamed x2 -> x8, local copies, waits for them, and re-layouts: 3.9 us -> 4.18 us
where the time goes in v3:
time: 58.5 us; the launch traced here: 58.4 us
  Pallas kernels  53.5 us (91%)
  local copies, waits for them, and re-layouts  4.18 us (7%)
  between operations  0.65 us (1%)
    pallas_call x1, Pallas kernels, shards(): pl.pallas_call(functools.partial(kernel, row_axis, col_axis, devices, col...  53.5 us
    unnamed x8, local copies, waits for them, and re-layouts  4.18 us

profile of v3, /device:TPU:16, one launch (start us, length us, event | category | flops | bytes accessed | tf_op | source)
XLA Modules:
  0.0 58.4 jit_solution(1549132898101115351)
XLA Ops:
  0.6 0.0 copy-start
  0.6 1.1 %copy-done = bf16[512,768]{1,0:T(8,128)(2,1)S(1)} copy-done((bf16[512,768]{1,0:T(8,128)(2,1)S(1)}, bf16[512,768]{1,0:T(8,128)(2,1)}, u32[]{:S(2)}) %copy-start) | copy-done | bytes 786456
  1.8 0.0 copy-start.1
  1.8 0.7 %copy-done.1 = s32[512]{0:T(512)S(1)} copy-done((s32[512]{0:T(512)S(1)}, s32[512]{0:T(512)}, u32[]{:S(2)}) %copy-start.1) | copy-done | bytes 2072
  2.4 0.0 copy-start.2
  2.4 0.7 %copy-done.2 = s32[64]{0:T(128)S(1)} copy-done((s32[64]{0:T(128)S(1)}, s32[64]{0:T(128)}, u32[]{:S(2)}) %copy-start.2) | copy-done | bytes 280
  3.1 53.5 %shard_map.50 = (f32[512,768]{1,0:T(8,128)S(1)}, f32[1,512]{1,0:T(1,128)S(1)}) custom-call(s32[64]{0:T(128)S(1)} %copy-done.2, bf16[512,768]{1,0:T(8,128)(2,1)S(1)} %copy-done, s32[1,512]{1,0:T(1,128)S(1)} %bitcast.2), custom_call_target="tpu_custom_call" | custom-call | tf_op jit(solution)/shard_map/pallas_call | solution.py:341
  56.6 0.6 copy.7
  57.2 1.1 %copy.8 = f32[512,768]{1,0:T(8,128)} copy(f32[512,768]{1,0:T(8,128)S(1)} %get-tuple-element.9) | data formatting | bytes 3145728
Async XLA Ops:
  0.6 1.1 %copy-start = (bf16[512,768]{1,0:T(8,128)(2,1)S(1)}, bf16[512,768]{1,0:T(8,128)(2,1)}, u32[]{:S(2)}) copy-start(bf16[512,768]{1,0:T(8,128)(2,1)} %e_ref.1) | copy-start | bytes 2359300
  1.8 0.7 %copy-start.1 = (s32[512]{0:T(512)S(1)}, s32[512]{0:T(512)}, u32[]{:S(2)}) copy-start(s32[512]{0:T(512)} %param.5) | copy-start | bytes 6148
  2.4 0.7 %copy-start.2 = (s32[64]{0:T(128)S(1)}, s32[64]{0:T(128)}, u32[]{:S(2)}) copy-start(s32[64]{0:T(128)} %cluster_ref.1) | copy-start | bytes 772

commit v4 on v3

--- a/solution.py
+++ b/solution.py
@@ -268,7 +268,7 @@
     turned = both.T
     lse_send[...] = turned[:8, :]
     lse_far[4] = turned[:8, :]
-    loss_ref[...] = turned[8:9, :]
+    loss_ref[...] = turned[8]
 
     def lse_copy(offset):
         return pltpu.make_async_remote_copy(
@@ -293,23 +293,33 @@
             w = w - (qrow_ref[0:1, h * BLOCK:(h + 1) * BLOCK] == line).astype(F32)
         weights[:, k * BLOCK:(k + 1) * BLOCK] = w.astype(jnp.bfloat16)
 
+    width = e_ref.shape[1]
+
+    def part_of(first, many, columns):
+        near = buf[pl.ds(pl.multiple_of((2 * g + 1 + first) * BLOCK, BLOCK), many * BLOCK), columns]
+        left = weights[:, first * BLOCK:(first + many) * BLOCK]
+        return jnp.dot(left, near, preferred_element_type=F32)
+
+    def own_product(t, carry):
+        columns = pl.ds(pl.multiple_of(t * 256, 256), 256)
+        grad_ref[:, columns] = part_of(7, 2, columns)
+        return carry
+
+    def rest_product(t, carry):
+        columns = pl.ds(pl.multiple_of(t * 256, 256), 256)
+        rest = part_of(0, 7, columns) + part_of(9, 7, columns)
+        grad_ref[:, columns] = (grad_ref[:, columns] + rest) * scale
+        return carry
+
     fill(7)
     fill(8)
+    lax.fori_loop(0, width // 256, own_product, 0)
     for offset in (-1, 1, -2, 2, -3, 3, -4, 4):
         when(exists(me + offset), lambda: lse_copy(-offset).wait_recv())
         for k in range(16):
             if (k - 7) // 2 == offset:
                 fill(k)
-
-    width = e_ref.shape[1]
-
-    def product(t, carry):
-        columns = pl.ds(pl.multiple_of(t * 256, 256), 256)
-        near = buf[pl.ds(pl.multiple_of((2 * g + 1) * BLOCK, BLOCK), 16 * BLOCK), columns]
-        grad_ref[:, columns] = jnp.dot(weights[...], near, preferred_element_type=F32) * scale
-        return carry
-
-    lax.fori_loop(0, width // 256, product, 0)
+    lax.fori_loop(0, width // 256, rest_product, 0)
 
     for offset in (-4, 4, -3, 3, -2, 2, -1, 1):
         when(exists(me + offset), lambda: lse_copy(offset).wait_send())
@@ -342,7 +352,7 @@
             functools.partial(kernel, row_axis, col_axis, devices, cols, width ** (-0.5)),
             out_shape=(
                 jax.ShapeDtypeStruct((rows, width), F32),
-                jax.ShapeDtypeStruct((1, rows), F32),
+                jax.ShapeDtypeStruct((rows,), F32),
             ),
             in_specs=[pl.BlockSpec(memory_space=pltpu.SMEM), vmem, vmem],
             out_specs=(vmem, vmem),
@@ -370,7 +380,7 @@
                 collective_id=0, has_side_effects=True, vmem_limit_bytes=34 * 1024 * 1024
             ),
         )(block_cluster, embeddings, partner_shift.reshape(1, rows))
-        return loss.reshape(rows), grad
+        return loss, grad
 
     in_specs = (P((row_axis, col_axis), None), P(), P((row_axis, col_axis)))
     out_specs = (P((row_axis, col_axis)), P((row_axis, col_axis), None))

time: 58.5 us -> 58.2 us (level)
  no operation moved by 1% of the time
where the time goes in v4:
time: 58.2 us; the launch traced here: 58 us
  Pallas kernels  53.1 us (91%)
  local copies, waits for them, and re-layouts  4.18 us (7%)
  between operations  0.65 us (1%)
    pallas_call x1, Pallas kernels, shards(): pl.pallas_call(functools.partial(kernel, row_axis, col_axis, devices, col...  53.1 us
    unnamed x8, local copies, waits for them, and re-layouts  4.18 us

profile of v4, /device:TPU:16, one launch (start us, length us, event | category | flops | bytes accessed | tf_op | source)
XLA Modules:
  0.0 58.0 jit_solution(792214164556928657)
XLA Ops:
  0.6 0.0 copy-start
  0.6 1.1 %copy-done = bf16[512,768]{1,0:T(8,128)(2,1)S(1)} copy-done((bf16[512,768]{1,0:T(8,128)(2,1)S(1)}, bf16[512,768]{1,0:T(8,128)(2,1)}, u32[]{:S(2)}) %copy-start) | copy-done | bytes 786456
  1.8 0.0 copy-start.1
  1.8 0.7 %copy-done.1 = s32[512]{0:T(512)S(1)} copy-done((s32[512]{0:T(512)S(1)}, s32[512]{0:T(512)}, u32[]{:S(2)}) %copy-start.1) | copy-done | bytes 2072
  2.4 0.0 copy-start.2
  2.4 0.7 %copy-done.2 = s32[64]{0:T(128)S(1)} copy-done((s32[64]{0:T(128)S(1)}, s32[64]{0:T(128)}, u32[]{:S(2)}) %copy-start.2) | copy-done | bytes 280
  3.1 53.1 %shard_map.50 = (f32[512,768]{1,0:T(8,128)S(1)}, f32[512]{0:T(512)S(1)}) custom-call(s32[64]{0:T(128)S(1)} %copy-done.2, bf16[512,768]{1,0:T(8,128)(2,1)S(1)} %copy-done, s32[1,512]{1,0:T(1,128)S(1)} %bitcast.1), custom_call_target="tpu_custom_call" | custom-call | tf_op jit(solution)/shard_map/pallas_call | solution.py:351
  56.2 0.6 %copy.7 = f32[512]{0:T(512)} copy(f32[512]{0:T(512)S(1)} %get-tuple-element.8) | data formatting | bytes 4096
  56.8 1.1 %copy.8 = f32[512,768]{1,0:T(8,128)} copy(f32[512,768]{1,0:T(8,128)S(1)} %get-tuple-element.9) | data formatting | bytes 3145728
Async XLA Ops:
  0.6 1.1 %copy-start = (bf16[512,768]{1,0:T(8,128)(2,1)S(1)}, bf16[512,768]{1,0:T(8,128)(2,1)}, u32[]{:S(2)}) copy-start(bf16[512,768]{1,0:T(8,128)(2,1)} %e_ref.1) | copy-start | bytes 2359300
  1.8 0.7 %copy-start.1 = (s32[512]{0:T(512)S(1)}, s32[512]{0:T(512)}, u32[]{:S(2)}) copy-start(s32[512]{0:T(512)} %param.5) | copy-start | bytes 6148
  2.4 0.7 %copy-start.2 = (s32[64]{0:T(128)S(1)}, s32[64]{0:T(128)}, u32[]{:S(2)}) copy-start(s32[64]{0:T(128)} %cluster_ref.1) | copy-start | bytes 772
